TPU v7x, 256 devices: a whole 4x4x8 slice. The times are simulated.
256 devices in a mesh: tmpl: 8 (over z), dp: 8 (over y, core), mp: 4 (over x).
Axes of the slice: x: 4, y: 4, z: 8, core: 2. Of those that a mesh axis runs over, the one named last changes fastest.
Arguments:
- hidden: bfloat16 [8, 32, 8, 8192], P('tmpl', ('dp', 'mp')), as said below
- norm_gain: float32 [8192], replicated, may hold values from 0.5 to 1.5
- head_weight: bfloat16 [152064, 8192], P(('tmpl', 'dp', 'mp'))
- lengths: int32 [32, 4], P(('dp', 'mp')), may hold values from 1 to 2, as said below
- targets: int32 [32, 4, 2], P(('dp', 'mp')), may hold values from 0 to 152063
- destinations: int32 [32, 4], P(('dp', 'mp')), may hold values from 0 to 7, as said below
Outputs:
- packed_logprobs: float32 [1536], P(('tmpl', 'dp', 'mp'))
- row_loglik: float32 [8, 32, 4], P('tmpl', ('dp', 'mp'))
- scores: float32 [32, 4], P(('dp', 'mp'))
Inputs may be any that keep to these rules, and one draw needn't show every extreme that they name: `lengths`: lengths and destinations hold for every template. For each index of mp and each destination j, the rows with destination j on the devices of that mp index hold exactly 6 tokens together; some row has 2 tokens. `destinations`: A device has at most 1 row with the same destination, and exactly 1 with some destination. `hidden`: slots beyond a row's length are read by no output.
All inputs are finite; a program needn't handle non-finite values.
Results may differ from a plain program's by a relative error of at most 0.0003.
Values may be sent and summed in bfloat16 or wider, within the bound.
No kernel may reach another device: no remote copies, remote signals or barrier semaphores. Data moves between devices by JAX's collectives and lax.ppermute only.
A program may use at most 192 MiB of HBM per device.

v0:
```python
import math
import jax
import jax.numpy as jnp
from jax import lax
from jax.sharding import Mesh
from jax.sharding import PartitionSpec as P

DP = ("dp_0", "dp_1")
TMPL_DP_MP = ("tmpl", "dp_0", "dp_1", "mp")
TMPL_DP = ("tmpl", "dp_0", "dp_1")
DP_MP = ("dp_0", "dp_1", "mp")


def side_by_side(arrays, axis, split_dim, concat_dim, along):
    ends, at = ([], 0)
    for a in arrays[:-1]:
        at += a.shape[along]
        ends.append(at)
    both = jnp.concatenate(arrays, axis=along)
    return tuple(
        jnp.split(
            lax.all_to_all(both, axis, split_axis=split_dim, concat_axis=concat_dim, tiled=True),
            ends,
            axis=along,
        )
    )


def in_order(parts, dim):
    shape = list(parts.shape[1:])
    shape[dim] *= parts.shape[0]
    return jnp.moveaxis(parts, 0, dim).reshape(shape)


def sent_to_all(value, axis):
    copies = jnp.broadcast_to(value, (lax.axis_size(axis), *value.shape))
    return lax.all_to_all(copies, axis, split_axis=0, concat_axis=0, tiled=True)


def gathered_copies(value, axis, dim):
    return in_order(sent_to_all(value, axis), dim)


def all_in_one(value, axis):
    leaves = jax.tree.leaves(value)
    order = sorted(range(len(leaves)), key=lambda k: -leaves[k].size)
    width = (1, *leaves[order[0]].shape)[-1]
    lines = [
        jnp.pad(leaves[k].reshape(-1), (0, -leaves[k].size % width)).reshape(-1, width)
        for k in order
    ]
    both, at, found = (lax.all_gather(jnp.concatenate(lines), axis), 0, {})
    for k, line in zip(order, lines):
        slab = both[:, at : at + len(line)].reshape(len(both), -1)
        found[k] = slab[:, : leaves[k].size].reshape(-1, *leaves[k].shape)
        at += len(line)
    numbers = iter(range(len(leaves)))
    return jax.tree.map(lambda _: found[next(numbers)], value)


def combined_by_axis(value, axes, combine):
    for axis in axes:
        pieces = all_in_one(value, axis)
        value = jax.tree.map(lambda part: part[0], pieces)
        for k in range(1, lax.axis_size(axis)):
            value = combine(value, jax.tree.map(lambda part: part[k], pieces))
    return value


def all_in_one_2(value, axis):
    leaves = jax.tree.leaves(value)
    order = sorted(range(len(leaves)), key=lambda k: -leaves[k].size)
    width = (1, *leaves[order[0]].shape)[-1]
    lines = [
        jnp.pad(leaves[k].reshape(-1), (0, -leaves[k].size % width)).reshape(-1, width)
        for k in order
    ]
    both, at, found = (sent_to_all(jnp.concatenate(lines), axis), 0, {})
    for k, line in zip(order, lines):
        slab = both[:, at : at + len(line)].reshape(len(both), -1)
        found[k] = slab[:, : leaves[k].size].reshape(-1, *leaves[k].shape)
        at += len(line)
    numbers = iter(range(len(leaves)))
    return jax.tree.map(lambda _: found[next(numbers)], value)


def collected_alike(value, axis):
    leaves, found = (jax.tree.leaves(value), {})
    for first, a in enumerate(leaves):
        if first not in found:
            alike = [k for k, b in enumerate(leaves) if b.dtype == a.dtype]
            got = (
                all_in_one_2([leaves[k] for k in alike], axis)
                if len(alike) > 1
                else [sent_to_all(a, axis)]
            )
            for k, b in zip(alike, got):
                found[k] = b
    numbers = iter(range(len(leaves)))
    return jax.tree.map(lambda _: found[next(numbers)], value)


def joined_by_halves(pieces, combine):
    while len(jax.tree.leaves(pieces)[0]) > 1:
        pieces = jax.vmap(combine)(
            *(jax.tree.map(lambda part: part[side::2], pieces) for side in (0, 1))
        )
    return jax.tree.map(lambda part: part[0], pieces)


def joined_all(value, axis, combine):
    pieces = collected_alike(value, axis)
    return joined_by_halves(pieces, combine)


def join_stats(first, second):
    highest = jnp.maximum(first[0], second[0])
    summed = first[1] * jnp.exp(first[0] - highest) + second[1] * jnp.exp(second[0] - highest)
    return (highest, summed, first[2] + second[2])


def join_templates(first, second):
    highest = jnp.maximum(first[0], second[0])
    summed = first[1] * jnp.exp(first[0] - highest) + second[1] * jnp.exp(second[0] - highest)
    return (highest, summed)


def on_device(hidden, norm_gain, head_weight, lengths, targets, destinations):
    width = hidden.shape[-1]
    row_count = lengths.shape[0] * lengths.shape[1]
    span_len = targets.shape[-1]
    dp_count = lax.axis_size(DP)
    pair_rows = max(1, row_count // dp_count)
    capacity = row_count * 3 // 2
    slot_count = pair_rows * span_len
    tokens = hidden.reshape(row_count * span_len, width).astype(jnp.float32)
    meansq = jnp.mean(tokens * tokens, axis=1, keepdims=True)
    normed = (tokens * lax.rsqrt(meansq + 1e-06) * norm_gain).astype(jnp.bfloat16)
    row_len = lengths.reshape(row_count)
    row_dest = destinations.reshape(row_count)
    token_target = targets.reshape(row_count * span_len)
    position = jnp.arange(span_len, dtype=jnp.int32)
    live = (position[None, :] < row_len[:, None]).reshape(-1)
    dest_hot = (row_dest[:, None] == jnp.arange(dp_count, dtype=jnp.int32)[None, :]).astype(
        jnp.int32
    )
    earlier = jnp.cumsum(dest_hot, axis=0) - dest_hot
    row_rank = jnp.sum(earlier * dest_hot, axis=1)
    token_slot = (
        (row_dest * slot_count + row_rank * span_len)[:, None] + position[None, :]
    ).reshape(-1)
    send_hot = (
        jnp.arange(dp_count * slot_count, dtype=jnp.int32)[:, None] == token_slot[None, :]
    ) & live[None, :]
    send_rows = jnp.dot(
        send_hot.astype(jnp.bfloat16), normed, preferred_element_type=jnp.float32
    ).astype(jnp.bfloat16)
    send_rows = send_rows.reshape(dp_count, slot_count, width)
    send_target = jnp.sum(jnp.where(send_hot, token_target[None, :], 0), axis=1).reshape(
        dp_count, slot_count
    )
    row_slot = row_dest * pair_rows + row_rank
    send_len = jnp.sum(
        jnp.where(
            jnp.arange(dp_count * pair_rows, dtype=jnp.int32)[:, None] == row_slot[None, :],
            row_len[None, :],
            0,
        ),
        axis=1,
    )
    send_len = send_len.reshape(dp_count, pair_rows)
    got_rows, got_target, got_len = (
        lax.all_to_all(send_rows, DP, split_axis=0, concat_axis=0, tiled=True),
        *side_by_side((send_target, send_len), DP, 0, 0, 1),
    )
    flat_len = got_len.reshape(-1)
    row_start = jnp.cumsum(flat_len) - flat_len
    place = (row_start[:, None] + position[None, :]).reshape(-1)
    used = (position[None, :] < flat_len[:, None]).reshape(-1)
    keep_hot = (jnp.arange(capacity, dtype=jnp.int32)[:, None] == place[None, :]) & used[None, :]
    balanced = jnp.dot(
        keep_hot.astype(jnp.bfloat16),
        got_rows.reshape(-1, width),
        preferred_element_type=jnp.float32,
    ).astype(jnp.bfloat16)
    balanced_target = jnp.sum(jnp.where(keep_hot, got_target.reshape(-1)[None, :], 0), axis=1)
    my_index = lax.axis_index(TMPL_DP_MP)
    vocab_ids = my_index * head_weight.shape[0] + jnp.arange(head_weight.shape[0], dtype=jnp.int32)
    near_rows, near_target = (
        gathered_copies(balanced, "mp", 0),
        gathered_copies(balanced_target, "mp", 0),
    )
    every_rows, every_target = (
        lax.all_gather(near_rows, TMPL_DP, axis=0, tiled=True),
        lax.all_gather(near_target, TMPL_DP, axis=0, tiled=True),
    )
    logits = lax.dot_general(
        every_rows, head_weight, (((1,), (1,)), ((), ())), preferred_element_type=jnp.float32
    )
    row_high = jnp.max(logits, axis=1)
    row_summed = jnp.sum(jnp.exp(logits - row_high[:, None]), axis=1)
    picked = jnp.sum(jnp.where(vocab_ids[None, :] == every_target[:, None], logits, 0.0), axis=1)
    own_start = my_index * capacity
    merged = combined_by_axis((row_high, row_summed, picked), TMPL_DP_MP, join_stats)
    own_high = lax.dynamic_slice_in_dim(merged[0], own_start, capacity)
    own_summed = lax.dynamic_slice_in_dim(merged[1], own_start, capacity)
    own_picked = lax.dynamic_slice_in_dim(merged[2], own_start, capacity)
    token_logprob = own_picked - own_high - jnp.log(own_summed)
    back_vals = jnp.sum(jnp.where(keep_hot, token_logprob[:, None], 0.0), axis=0).reshape(
        dp_count, slot_count
    )
    returned = lax.all_to_all(back_vals, DP, split_axis=0, concat_axis=0, tiled=True)
    token_vals = jnp.sum(jnp.where(send_hot, returned.reshape(-1)[:, None], 0.0), axis=0)
    row_loglik = jnp.sum(token_vals.reshape(row_count, span_len), axis=1)
    highest, summed = joined_all((row_loglik, jnp.ones_like(row_loglik)), "tmpl", join_templates)
    scores = highest + jnp.log(summed) - math.log(lax.axis_size("tmpl"))
    return (token_logprob, row_loglik.reshape((1,) + lengths.shape), scores.reshape(lengths.shape))


def solution(mesh):
    torus = Mesh(
        mesh.devices.reshape(mesh.shape["tmpl"], 4, 2, mesh.shape["mp"]),
        ("tmpl", "dp_0", "dp_1", "mp"),
    )
    in_specs = (
        P("tmpl", DP_MP, None, None),
        P(),
        P(TMPL_DP_MP, None),
        P(DP_MP, None),
        P(DP_MP, None, None),
        P(DP_MP, None),
    )
    out_specs = (P(TMPL_DP_MP), P("tmpl", DP_MP, None), P(DP_MP, None))
    return jax.shard_map(
        on_device, mesh=torus, in_specs=in_specs, out_specs=out_specs, check_vma=False
    )
```

profile of v0, /device:TPU:2, one launch (start us, length us, event | category | flops | bytes accessed | tf_op | source)
XLA Modules:
  0.0 272.0 jit_solution(1676549541065805954)
XLA Ops:
  7.2 0.7 fusion.62
  7.9 0.8 select_reduce_fusion.6
  8.8 0.7 add_multiply_fusion
  9.4 0.7 fusion.77
  10.3 0.7 iota_compare_fusion.4
  11.1 0.7 select_reduce_fusion.5
  11.9 0.8 copy.29
  12.9 0.7 pad_add_fusion
  13.6 4.5 %all-to-all-start = ((s32[8,1,3]{2,1,0:T(1,128)}), s32[8,1,3]{2,1,0:T(1,128)S(1)}, u32[]{:S(2)}, u32[]{:S(2)}) async-start(s32[8,1,3]{2,1,0:T(1,128)} %bitcast.53), calls=%async_computation | async-start | bytes 8192 | tf_op jit(solution)/shard_map/all_to_all | solution.py:22
  18.1 1.1 fusion
  19.2 1.3 convolution_convert_fusion
  20.4 0.9 reshape.1033
  21.3 2.1 all-to-all-done
  23.4 3.4 %all-to-all-start.1 = ((bf16[8,2,8192]{2,1,0:T(2,128)(2,1)}), bf16[8,2,8192]{2,1,0:T(2,128)(2,1)S(1)}, u32[]{:S(2)}, u32[]{:S(2)}) async-start(bf16[8,2,8192]{2,1,0:T(2,128)(2,1)} %reshape.1033), calls=%async_computation.1 | async-start | bytes 524288 | tf_op jit(solution)/shard_map/all_to_all | solution.py:173
  26.9 0.2 reduce-window.4
  27.4 6.8 %all-to-all-done.1 = bf16[8,2,8192]{2,1,0:T(2,128)(2,1)S(1)} async-done(((bf16[8,2,8192]{2,1,0:T(2,128)(2,1)}), bf16[8,2,8192]{2,1,0:T(2,128)(2,1)S(1)}, u32[]{:S(2)}, u32[]{:S(2)}) %all-to-all-start.1) | async-done | bytes 262176 | tf_op jit(solution)/shard_map/all_to_all | solution.py:173
  34.2 0.1 reshape.1034
  34.3 0.2 convolution_convert_fusion.1
  34.5 12.3 %all_to_all.42 = bf16[4,6,8192]{2,1,0:T(8,128)(2,1)S(1)} all-to-all(bf16[4,6,8192]{2,1,0:T(8,128)(2,1)S(1)} %broadcast_in_dim.101), channel_id=1, replica_groups=mesh['tmpl'=8,'dp_0'=4,'dp_1'=2,'mp'=4] {'mp'}, dimensions={0} | all-to-all | bytes 786432 | tf_op jit(solution)/shard_map/all_to_all | solution.py:37
  46.8 0.9 reshape.1035
  47.8 0.6 dynamic-slice.1
  49.2 0.1 select_reduce_fusion.3
  49.3 0.6 broadcast_in_dim.105
  49.9 4.6 %all-to-all-start.3 = ((s32[4,1,6]{2,1,0:T(1,128)}), s32[4,1,6]{2,1,0:T(1,128)S(1)}, u32[]{:S(2)}, u32[]{:S(2)}) async-start(s32[4,1,6]{2,1,0:T(1,128)} %broadcast_in_dim.105), calls=%async_computation.3 | async-start | bytes 4096 | tf_op jit(solution)/shard_map/all_to_all | solution.py:37
  54.5 3.8 %all-to-all-done.3 = s32[4,1,6]{2,1,0:T(1,128)S(1)} async-done(((s32[4,1,6]{2,1,0:T(1,128)}), s32[4,1,6]{2,1,0:T(1,128)S(1)}, u32[]{:S(2)}, u32[]{:S(2)}) %all-to-all-start.3) | async-done | bytes 128 | tf_op jit(solution)/shard_map/all_to_all | solution.py:37
  58.4 0.5 broadcast.89
  58.9 0.7 reduce.22
  59.6 0.2 dynamic-update-slice
  59.9 22.7 %all-reduce.1 = s32[1536]{0:T(1024)S(1)} all-reduce(s32[1536]{0:T(1024)S(1)} %dynamic-update-slice), channel_id=1, replica_groups=mesh['tmpl'=8,'dp_0'=4,'dp_1'=2,'mp'=4] {'tmpl','dp_0','dp_1'}, use_global_device_ids=true, to_apply=%add.1 | all-reduce | flops 1536 | bytes 12288
  82.6 86.2 %all-gather.10.cloned.1.call-done = bf16[1536,8192]{1,0:T(8,128)(2,1)} async-done(((bf16[24,8192]{1,0:T(8,128)(2,1)}), bf16[1536,8192]{1,0:T(8,128)(2,1)}) %all-gather.10.cloned.1.call-update) | async-done | bytes 25165840 | tf_op jit(solution)/shard_map/all_gather | solution.py:194
  168.7 21.1 %fusion.84 = (f32[1536]{0:T(1024)S(1)}, f32[1536,594]{0,1:T(8,128)S(1)}) fusion(bf16[1536,8192]{1,0:T(8,128)(2,1)} %all-gather.10.cloned.1.call-done, bf16[594,8192]{1,0:T(8,128)(2,1)} %param.8), kind=kOutput, calls=%fused_computation.174 | convolution fusion | flops 14949410816 | bytes 38553600 | tf_op jit(solution)/shard_map/dot_general | solution.py:197
  189.9 0.9 exponential_reduce_fusion
  190.8 24.7 %all-gather.4 = f32[8,3,1536]{2,1,0:T(4,128)S(1)} all-gather(f32[1,3,1536]{2,1,0:T(4,128)S(1)} %maximum_bitcast_fusion), channel_id=2, replica_groups=mesh['tmpl'=8,'dp_0'=4,'dp_1'=2,'mp'=4] {'tmpl'}, dimensions={0}, use_global_device_ids=true | all-gather | bytes 165888 | tf_op jit(solution)/shard_map/all_gather | solution.py:52
  215.5 0.1 fusion.23
  215.7 11.9 %all-gather.5 = f32[4,3,1536]{2,1,0:T(4,128)S(1)} all-gather(f32[1,3,1536]{2,1,0:T(4,128)S(1)} %maximum_bitcast_fusion.1), channel_id=3, replica_groups=mesh['tmpl'=8,'dp_0'=4,'dp_1'=2,'mp'=4] {'dp_0'}, dimensions={0}, use_global_device_ids=true | all-gather | bytes 92160 | tf_op jit(solution)/shard_map/all_gather | solution.py:52
  227.8 1.8 all-gather.6
  229.7 11.9 %all-gather.7 = f32[4,3,1536]{2,1,0:T(4,128)S(1)} all-gather(f32[1,3,1536]{2,1,0:T(4,128)S(1)} %maximum_bitcast_fusion.3), channel_id=5, replica_groups=mesh['tmpl'=8,'dp_0'=4,'dp_1'=2,'mp'=4] {'mp'}, dimensions={0}, use_global_device_ids=true | all-gather | bytes 92160 | tf_op jit(solution)/shard_map/all_gather | solution.py:52
  241.6 0.1 fusion.82
  241.8 0.1 fusion.76
  242.1 7.8 %all_to_all.43 = f32[8,1,2]{2,1,0:T(1,128)S(1)} all-to-all(f32[8,1,2]{2,1,0:T(1,128)S(1)} %bitcast.310), channel_id=1, replica_groups=mesh['tmpl'=8,'dp_0'=4,'dp_1'=2,'mp'=4] {'dp_0','dp_1'}, dimensions={0} | all-to-all | bytes 128 | tf_op jit(solution)/shard_map/all_to_all | solution.py:212
  249.9 0.5 broadcast.90
  250.4 0.7 reduce.23
  251.2 0.2 select_reduce_fusion.1
  251.5 0.1 reduce_sum.102
  251.6 11.8 %all_to_all.44 = f32[8,2,4]{2,1,0:T(2,128)S(1)} all-to-all(f32[8,2,4]{2,1,0:T(2,128)S(1)} %broadcast_in_dim.112), channel_id=1, replica_groups=mesh['tmpl'=8,'dp_0'=4,'dp_1'=2,'mp'=4] {'tmpl'}, dimensions={0} | all-to-all | bytes 512 | tf_op jit(solution)/shard_map/all_to_all | solution.py:37
  263.6 0.1 slice.391
  263.8 0.1 slice.384
  264.5 0.6 copy.38
  (63 shorter events, 2.9 us)
Async XLA Ops:
  7.2 40.6 %copy-start.2 = (u32[256]{0:T(256)S(1)}, u32[256]{0:T(256)}, u32[]{:S(2)}) copy-start(u32[256]{0:T(256)} %constant.64) | copy-start | bytes 3076
  13.6 9.8 %all-to-all-start = ((s32[8,1,3]{2,1,0:T(1,128)}), s32[8,1,3]{2,1,0:T(1,128)S(1)}, u32[]{:S(2)}, u32[]{:S(2)}) async-start(s32[8,1,3]{2,1,0:T(1,128)} %bitcast.53), calls=%async_computation | async-start | bytes 8192 | tf_op jit(solution)/shard_map/all_to_all | solution.py:22
  23.4 10.8 %all-to-all-start.1 = ((bf16[8,2,8192]{2,1,0:T(2,128)(2,1)}), bf16[8,2,8192]{2,1,0:T(2,128)(2,1)S(1)}, u32[]{:S(2)}, u32[]{:S(2)}) async-start(bf16[8,2,8192]{2,1,0:T(2,128)(2,1)} %reshape.1033), calls=%async_computation.1 | async-start | bytes 524288 | tf_op jit(solution)/shard_map/all_to_all | solution.py:173
  26.8 141.9 %all-gather.10.cloned.1.call-start = ((), (), s32[]{:S(2)}) async-start(), calls=%async_computation.6 | async-start | bytes 25559040 | tf_op jit(solution)/shard_map/all_gather | solution.py:194
  49.9 8.4 %all-to-all-start.3 = ((s32[4,1,6]{2,1,0:T(1,128)}), s32[4,1,6]{2,1,0:T(1,128)S(1)}, u32[]{:S(2)}, u32[]{:S(2)}) async-start(s32[4,1,6]{2,1,0:T(1,128)} %broadcast_in_dim.105), calls=%async_computation.3 | async-start | bytes 4096 | tf_op jit(solution)/shard_map/all_to_all | solution.py:37
  241.9 23.2 %copy-start = (f32[6]{0:T(128)}, f32[6]{0:T(128)S(1)}, u32[]{:S(2)}) copy-start(f32[6]{0:T(128)S(1)} %fusion.76) | copy-start | bytes 76
  251.6 13.6 %copy-start.1 = (f32[4]{0:T(128)}, f32[4]{0:T(128)S(1)}, u32[]{:S(2)}) copy-start(f32[4]{0:T(128)S(1)} %reduce_sum.102) | copy-start | bytes 52
Sparse Core Ops, SparseCore 0:
  47.9 120.7 all-gather.9
where the time goes:
time: 273 us; the launch traced here: 272 us
  blocking collectives  105 us (38%)
  waiting for transfers between devices  98.9 us (36%)
  matrix products  22.5 us (8%)
  between operations  15 us (5%)
  starting transfers between devices  12.5 us (5%)
  other arithmetic  10 us (4%)
  local copies, waits for them, and re-layouts  8.07 us (3%)
    all_gather x1, waiting for transfers between devices, on_device(): lax.all_gather(near_rows, TMPL_DP, axis=0, tiled=True)  86.2 us
    all_gather x4, blocking collectives, all_in_one(): both, at, found = (lax.all_gather(jnp.concatenate(lines), axis), 0, {})  50.4 us
    all_to_all x2, blocking collectives, sent_to_all(): return lax.all_to_all(copies, axis, split_axis=0, concat_axis=0, tiled=True)  24.1 us
    unnamed x1, blocking collectives  22.7 us
    dot_general x1, matrix products, on_device(): lax.dot_general(every_rows, head_weight, (((1,), (1,)), ((), ())), prefer...  21.1 us
    all_to_all x1, blocking collectives, on_device(): lax.all_to_all(back_vals, DP, split_axis=0, concat_axis=0, tiled=True)  7.82 us
    all_to_all x1, waiting for transfers between devices, on_device(): lax.all_to_all(send_rows, DP, split_axis=0, concat_axis=0, tiled=True)  6.78 us
  transfers between devices with their start and end apart: 4, of which 4 were waited for; matrix products, arithmetic and copies ran while one was open for 2% of the time, Pallas kernels for 0%

commit v1 on v0

--- a/solution.py
+++ b/solution.py
@@ -191,7 +191,9 @@
         gathered_copies(balanced_target, "mp", 0),
     )
     every_rows, every_target = (
-        lax.all_gather(near_rows, TMPL_DP, axis=0, tiled=True),
+        jnp.concatenate(
+            lax.all_to_all(jnp.stack([near_rows] * lax.axis_size(TMPL_DP)), TMPL_DP, 0, 0), axis=0
+        ),
         lax.all_gather(near_target, TMPL_DP, axis=0, tiled=True),
     )
     logits = lax.dot_general(

time: 273 us -> 737 us (2.70)
  blocking collectives: 105 us -> 637 us
  waiting for transfers between devices: 98.9 us -> 19.9 us
  starting transfers between devices: 12.5 us -> 27.8 us
  between operations: 15 us -> 1.55 us
  local copies, waits for them, and re-layouts: 8.07 us -> 16.6 us
    unnamed x1, blocking collectives: 22.7 us -> 562 us
    all_gather x1 -> x0, waiting for transfers between devices: 86.2 us -> none  [on_device(): lax.all_gather(near_rows, TMPL_DP, axis=0, tiled=True)]
    all_to_all x2 -> x1, blocking collectives: 24.1 us -> 12.5 us  [sent_to_all(): return lax.all_to_all(copies, axis, split_axis=0, concat_axis=0, tiled=True)]
    all_to_all x0 -> x1, starting transfers between devices: none -> 10.4 us  [on_device(): lax.all_to_all(jnp.stack([near_rows] * lax.axis_size(TMPL_DP)), TMPL_DP,...]
    another operation x0 -> x2, local copies, waits for them, and re-layouts: none -> 8.72 us  [on_device(): jnp.stack([near_rows] * lax.axis_size(TMPL_DP))]
  transfers between devices with their start and end apart: 4 -> 5, of which waited for: 4 -> 4; matrix products, arithmetic and copies ran while one was open for 2% -> 1% of each run, Pallas kernels for 0% -> 0%
where the time goes in v1:
time: 737 us; the launch traced here: 735 us
  blocking collectives  637 us (86%)
  starting transfers between devices  27.8 us (4%)
  matrix products  22.5 us (3%)
  waiting for transfers between devices  19.9 us (3%)
  local copies, waits for them, and re-layouts  16.6 us (2%)
  other arithmetic  10 us (1%)
    unnamed x1, blocking collectives  562 us
    all_gather x4, blocking collectives, all_in_one(): both, at, found = (lax.all_gather(jnp.concatenate(lines), axis), 0, {})  52.4 us
    dot_general x1, matrix products, on_device(): lax.dot_general(every_rows, head_weight, (((1,), (1,)), ((), ())), prefer...  21.1 us
  transfers between devices with their start and end apart: 5, of which 4 were waited for; matrix products, arithmetic and copies ran while one was open for 1% of the time, Pallas kernels for 0%

profile of v1, /device:TPU:2, one launch (start us, length us, event | category | flops | bytes accessed | tf_op | source)
XLA Modules:
  0.0 735.3 jit_solution(8146623075030684807)
XLA Ops:
  0.6 0.7 fusion.62
  1.4 0.8 select_reduce_fusion.6
  2.2 0.7 add_multiply_fusion
  2.9 0.7 fusion.77
  3.7 0.7 iota_compare_fusion.4
  4.5 0.7 select_reduce_fusion.5
  5.4 0.8 copy.29
  6.4 0.7 pad_add_fusion
  7.0 4.5 all-to-all-start
  11.5 1.1 fusion
  12.6 1.2 convolution_convert_fusion
  13.9 0.9 reshape.1035
  14.7 2.1 all-to-all-done
  16.8 3.4 all-to-all-start.1
  20.3 0.2 reduce-window.4
  20.8 6.8 all-to-all-done.1
  27.7 0.1 reshape.1036
  27.8 0.2 convolution_convert_fusion.1
  27.9 0.8 broadcast_in_dim.101
  28.8 4.8 all-to-all-start.2
  33.8 0.1 select_reduce_fusion.3
  33.9 7.4 %all-to-all-done.2 = bf16[4,6,8192]{2,1,0:T(8,128)(2,1)S(1)} async-done(((bf16[4,6,8192]{2,1,0:T(8,128)(2,1)}), bf16[4,6,8192]{2,1,0:T(8,128)(2,1)S(1)}, u32[]{:S(2)}, u32[]{:S(2)}) %all-to-all-start.2) | async-done | bytes 393248 | tf_op jit(solution)/shard_map/all_to_all | solution.py:37
  41.2 0.6 broadcast_in_dim.105
  41.8 4.7 all-to-all-start.4
  46.5 0.1 stack_reshape.2
  46.7 3.7 all-to-all-done.4
  50.3 8.6 %stack.3 = bf16[64,24,8192]{2,1,0:T(8,128)(2,1)} broadcast(bf16[24,8192]{1,0:T(8,128)(2,1)S(1)} %stack_reshape.2), dimensions={1,2} | broadcast | bytes 25559040 | tf_op jit(solution)/shard_map/stack | solution.py:195
  58.9 10.4 %all-to-all-start.3 = ((bf16[64,24,8192]{2,1,0:T(8,128)(2,1)}), bf16[64,24,8192]{2,1,0:T(8,128)(2,1)}, u32[]{:S(2)}, u32[]{:S(2)}) async-start(bf16[64,24,8192]{2,1,0:T(8,128)(2,1)} %stack.3), calls=%async_computation.3 | async-start | bytes 50331648 | tf_op jit(solution)/shard_map/all_to_all | solution.py:195
  69.4 0.6 dynamic-slice.1
  70.6 0.5 broadcast.90
  71.1 0.7 reduce.22
  71.9 0.2 dynamic-update-slice
  72.1 562.3 %all-reduce.1 = s32[1536]{0:T(1024)S(1)} all-reduce(s32[1536]{0:T(1024)S(1)} %dynamic-update-slice), channel_id=1, replica_groups=mesh['tmpl'=8,'dp_0'=4,'dp_1'=2,'mp'=4] {'tmpl','dp_0','dp_1'}, use_global_device_ids=true, to_apply=%add.1 | all-reduce | flops 1536 | bytes 12288
  634.4 21.1 %fusion.84 = (f32[1536]{0:T(1024)S(1)}, f32[1536,594]{0,1:T(8,128)S(1)}) fusion(bf16[1536,8192]{1,0:T(8,128)(2,1)} %bitcast.11, bf16[594,8192]{1,0:T(8,128)(2,1)} %param.8), kind=kOutput, calls=%fused_computation.174 | convolution fusion | flops 14949410816 | bytes 38553600 | tf_op jit(solution)/shard_map/dot_general | solution.py:199
  655.5 0.9 exponential_reduce_fusion
  656.5 26.2 %all-gather.4 = f32[8,3,1536]{2,1,0:T(4,128)S(1)} all-gather(f32[1,3,1536]{2,1,0:T(4,128)S(1)} %maximum_bitcast_fusion), channel_id=2, replica_groups=mesh['tmpl'=8,'dp_0'=4,'dp_1'=2,'mp'=4] {'tmpl'}, dimensions={0}, use_global_device_ids=true | all-gather | bytes 165888 | tf_op jit(solution)/shard_map/all_gather | solution.py:52
  682.7 0.1 fusion.23
  682.9 13.2 %all-gather.5 = f32[4,3,1536]{2,1,0:T(4,128)S(1)} all-gather(f32[1,3,1536]{2,1,0:T(4,128)S(1)} %maximum_bitcast_fusion.1), channel_id=3, replica_groups=mesh['tmpl'=8,'dp_0'=4,'dp_1'=2,'mp'=4] {'dp_0'}, dimensions={0}, use_global_device_ids=true | all-gather | bytes 92160 | tf_op jit(solution)/shard_map/all_gather | solution.py:52
  696.3 1.8 all-gather.6
  698.2 11.2 %all-gather.7 = f32[4,3,1536]{2,1,0:T(4,128)S(1)} all-gather(f32[1,3,1536]{2,1,0:T(4,128)S(1)} %maximum_bitcast_fusion.3), channel_id=5, replica_groups=mesh['tmpl'=8,'dp_0'=4,'dp_1'=2,'mp'=4] {'mp'}, dimensions={0}, use_global_device_ids=true | all-gather | bytes 92160 | tf_op jit(solution)/shard_map/all_gather | solution.py:52
  709.4 0.1 fusion.82
  709.8 9.6 %all_to_all.47 = f32[8,1,2]{2,1,0:T(1,128)S(1)} all-to-all(f32[8,1,2]{2,1,0:T(1,128)S(1)} %bitcast.311), channel_id=1, replica_groups=mesh['tmpl'=8,'dp_0'=4,'dp_1'=2,'mp'=4] {'dp_0','dp_1'}, dimensions={0} | all-to-all | bytes 128 | tf_op jit(solution)/shard_map/all_to_all | solution.py:214
  719.4 0.5 broadcast.91
  719.9 0.7 reduce.23
  720.6 0.2 select_reduce_fusion.1
  720.9 0.1 reduce_sum.102
  721.1 12.5 %all_to_all.48 = f32[8,2,4]{2,1,0:T(2,128)S(1)} all-to-all(f32[8,2,4]{2,1,0:T(2,128)S(1)} %broadcast_in_dim.112), channel_id=1, replica_groups=mesh['tmpl'=8,'dp_0'=4,'dp_1'=2,'mp'=4] {'tmpl'}, dimensions={0} | all-to-all | bytes 512 | tf_op jit(solution)/shard_map/all_to_all | solution.py:37
  734.6 0.6 copy.38
  (64 shorter events, 3.1 us)
Async XLA Ops:
  7.0 9.8 %all-to-all-start = ((s32[8,1,3]{2,1,0:T(1,128)}), s32[8,1,3]{2,1,0:T(1,128)S(1)}, u32[]{:S(2)}, u32[]{:S(2)}) async-start(s32[8,1,3]{2,1,0:T(1,128)} %bitcast.54), calls=%async_computation | async-start | bytes 8192 | tf_op jit(solution)/shard_map/all_to_all | solution.py:22
  16.8 10.8 %all-to-all-start.1 = ((bf16[8,2,8192]{2,1,0:T(2,128)(2,1)}), bf16[8,2,8192]{2,1,0:T(2,128)(2,1)S(1)}, u32[]{:S(2)}, u32[]{:S(2)}) async-start(bf16[8,2,8192]{2,1,0:T(2,128)(2,1)} %reshape.1035), calls=%async_computation.1 | async-start | bytes 524288 | tf_op jit(solution)/shard_map/all_to_all | solution.py:173
  28.8 12.5 %all-to-all-start.2 = ((bf16[4,6,8192]{2,1,0:T(8,128)(2,1)}), bf16[4,6,8192]{2,1,0:T(8,128)(2,1)S(1)}, u32[]{:S(2)}, u32[]{:S(2)}) async-start(bf16[4,6,8192]{2,1,0:T(8,128)(2,1)} %broadcast_in_dim.101), calls=%async_computation.2 | async-start | bytes 1048576 | tf_op jit(solution)/shard_map/all_to_all | solution.py:37
  41.8 8.5 %all-to-all-start.4 = ((s32[4,1,6]{2,1,0:T(1,128)}), s32[4,1,6]{2,1,0:T(1,128)S(1)}, u32[]{:S(2)}, u32[]{:S(2)}) async-start(s32[4,1,6]{2,1,0:T(1,128)} %broadcast_in_dim.105), calls=%async_computation.4 | async-start | bytes 4096 | tf_op jit(solution)/shard_map/all_to_all | solution.py:37
  58.9 10.5 %copy-start.2 = (u32[256]{0:T(256)S(1)}, u32[256]{0:T(256)}, u32[]{:S(2)}) copy-start(u32[256]{0:T(256)} %constant.64) | copy-start | bytes 3076
  58.9 575.5 %all-to-all-start.3 = ((bf16[64,24,8192]{2,1,0:T(8,128)(2,1)}), bf16[64,24,8192]{2,1,0:T(8,128)(2,1)}, u32[]{:S(2)}, u32[]{:S(2)}) async-start(bf16[64,24,8192]{2,1,0:T(8,128)(2,1)} %stack.3), calls=%async_computation.3 | async-start | bytes 50331648 | tf_op jit(solution)/shard_map/all_to_all | solution.py:195
  709.6 25.6 %copy-start = (f32[6]{0:T(128)}, f32[6]{0:T(128)S(1)}, u32[]{:S(2)}) copy-start(f32[6]{0:T(128)S(1)} %fusion.76) | copy-start | bytes 76
  721.0 14.2 %copy-start.1 = (f32[4]{0:T(128)}, f32[4]{0:T(128)S(1)}, u32[]{:S(2)}) copy-start(f32[4]{0:T(128)S(1)} %reduce_sum.102) | copy-start | bytes 52
